TPU v7x, 128 devices: a whole 4x4x4 slice. The times are simulated.
128 devices in a mesh: neuron: 16 (over z, y), trial: 8 (over x, core).
Axes of the slice: x: 4, y: 4, z: 4, core: 2. Of those that a mesh axis runs over, the one named last changes fastest.
Arguments:
- drive: bfloat16 [8, 128, 131072], P(None, 'trial', 'neuron'), may hold values from -6 to 6
- learning: bfloat16 [8, 128, 131072], P(None, 'trial', 'neuron'), may hold values from -6 to 6
- membrane_init: float32 [128, 131072], P('trial', 'neuron'), may hold values from -3 to 3
- adapt_init: float32 [128, 131072], P('trial', 'neuron'), may hold values from 0 to 1
- trace_init: float32 [128, 131072], P('trial', 'neuron'), may hold values from 0 to 3
- membrane_decay: float32 [131072], P('neuron'), may hold values from 0.6 to 0.95
- adapt_decay: float32 [131072], P('neuron'), may hold values from 0.8 to 0.99
- adapt_gain: float32 [131072], P('neuron'), may hold values from 0.2 to 1
- threshold: float32 [131072], P('neuron'), may hold values from 0.5 to 1.5
- left_factor: bfloat16 [131072, 512], P('neuron'), may hold values from -6 to 6
- right_factor: bfloat16 [131072, 512], P('neuron'), may hold values from -16 to 16
Outputs:
- left_new: bfloat16 [131072, 512], P(('neuron', 'trial'))
- right_new: bfloat16 [131072, 512], P(('neuron', 'trial'))
All inputs are finite; a program needn't handle non-finite values.
Results may differ from a plain program's by a relative error of at most 0.0085.
Values may be sent and summed in bfloat16 or wider, within the bound.
No kernel may reach another device: no remote copies, remote signals or barrier semaphores. Data moves between devices by JAX's collectives and lax.ppermute only.
A program may use at most 128 MiB of HBM per device.

v0:
```python
import math

import jax
import jax.numpy as jnp
from jax import lax
from jax.experimental import pallas as pl
from jax.experimental.pallas import tpu as pltpu
from jax.sharding import PartitionSpec as P

sharpness = 3.0
learn_rate = 0.5

f32 = jnp.float32
bf16 = jnp.bfloat16
highest = lax.Precision.HIGHEST
block = 128
loops = 2

NN = (((1,), (0,)), ((), ()))
NT = (((1,), (1,)), ((), ()))
TN = (((0,), (0,)), ((), ()))

vmem = pl.BlockSpec(memory_space=pltpu.VMEM)


def dot(a, b, dims, precision=None):
    return lax.dot_general(a, b, dims, precision=precision, preferred_element_type=f32)


def swap(values, axes):
    return lax.all_to_all(values, axes, split_axis=0, concat_axis=0, tiled=True)


def spread(values, axes):
    copies = math.prod(lax.axis_size(a) for a in ((axes,) if isinstance(axes, str) else axes))
    return swap(jnp.broadcast_to(values[None], (copies,) + values.shape), axes)


def fire(membrane, adaptation, gain, threshold):
    level = membrane - threshold - gain * adaptation
    return 0.5 * jnp.tanh((0.5 * sharpness) * level) + 0.5


def post(total, weight, out_ref):
    total = (total * weight).astype(bf16)
    for i in range(out_ref.shape[0]):
        out_ref[i] = total


def halves(value):
    high = value.astype(bf16)
    return high, (value - high.astype(f32)).astype(bf16)


def dot3(a, b, dims):
    return dot(a[0], b[0], dims) + (dot(a[0], b[1], dims) + dot(a[1], b[0], dims))


def fetch(src_ref, dst_ref, sems, pieces):
    rows = src_ref.shape[0] // pieces
    copies = [
        pltpu.make_async_copy(
            src_ref.at[pl.ds(c * rows, rows)], dst_ref.at[pl.ds(c * rows, rows)], sems.at[c]
        )
        for c in range(pieces)
    ]
    for copy in copies:
        copy.start()
    return copies


def start_kernel(
    weight, me_ref, gain_hbm, thr_hbm, mem_hbm, ada_hbm, right_hbm, drive_hbm, learn_hbm,
    spk_ref, out_ref, right_ref, drive_ref, learn_ref, gain_ref, thr_ref, mem_ref, ada_ref, sems, sems_more,
):
    pairs = (
        (gain_hbm, gain_ref), (thr_hbm, thr_ref), (mem_hbm, mem_ref), (ada_hbm, ada_ref),
        (drive_hbm, drive_ref), (learn_hbm, learn_ref),
    )
    more = [pltpu.make_async_copy(s, d, sems_more.at[i]) for i, (s, d) in enumerate(pairs)]
    for copy in more[:4]:
        copy.start()
    copies = fetch(right_hbm, right_ref, sems, 8)
    for copy in more[4:]:
        copy.start()
    for copy in more[:4]:
        copy.wait()
    count = len(copies)
    width = right_ref.shape[0] // count

    def several(i, total):
        for c in range(2):
            c = 2 * i + c
            at = pl.ds(pl.multiple_of(c * width, width), width)
            spikes = fire(mem_ref[:, at], ada_ref[:, at], gain_ref[:, at], thr_ref[:, at])
            spk_ref[:, at] = spikes
            pltpu.make_async_copy(right_hbm.at[at], right_ref.at[at], sems.at[c]).wait()
            total = total + dot(spikes.astype(bf16), right_ref[at, :], NN)
        return total

    total = jnp.zeros((mem_ref.shape[0], right_ref.shape[1]), f32)
    post(lax.fori_loop(0, count // 2, several, total), weight, out_ref)
    for copy in more[4:]:
        copy.wait()


def step_kernel(weight_n, weight_r, moment, steps, *refs):
    first, last = moment == 0, moment + 1 == steps
    (me_ref, in_ref, dec_ref, ad_ref, gain_ref, thr_ref, drive_ref, learn_ref, mem_ref, ada_ref, fil_ref,
     spk_ref, left_ref, right_ref) = refs[:14]
    outs = refs[14:] if first else refs[16:]
    sig_ref, pre_ref = outs[:2]
    if not last:
        mem_out, ada_out, fil_out, spk_out, out_ref = outs[2:7]
    pieces, _, width = sig_ref.shape
    trials = mem_ref.shape[0]
    rows = pl.ds(moment * trials, trials)
    if first:
        left_hbm, left_ref = left_ref, outs[7]
        sems = outs[8]
        fetch(left_hbm, left_ref, sems, pieces)
    projected = jnp.sum(in_ref[...].astype(f32), 0).astype(bf16)

    def piece(c, total):
        at = pl.ds(pl.multiple_of(c * width, width), width)
        decay, threshold = dec_ref[:, at], thr_ref[:, at]
        if first:
            pltpu.make_async_copy(left_hbm.at[at], left_ref.at[at], sems.at[c]).wait()
        current = dot(projected, left_ref[at, :], NT) * weight_r
        spikes = spk_ref[:, at]
        drive = drive_ref[moment, :, at].astype(f32)
        membrane = decay * mem_ref[:, at] + drive + current - threshold * spikes
        adaptation = ad_ref[:, at] * ada_ref[:, at] + spikes
        spikes = fire(membrane, adaptation, gain_ref[:, at], threshold)
        slope = sharpness * spikes * (1.0 - spikes)
        filtered = decay * fil_ref[:, at] + spikes
        slot = me_ref[0] ^ c
        sig_ref[c, rows] = (learn_ref[moment, :, at].astype(f32) * slope).astype(bf16)
        pre_ref[slot, rows] = filtered.astype(bf16)
        if last:
            return total
        mem_out[:, at] = membrane
        ada_out[:, at] = adaptation
        fil_out[:, at] = filtered
        spk_out[:, at] = spikes
        return total + dot(spikes.astype(bf16), right_ref[at, :], NN)

    total = jnp.zeros((trials, right_ref.shape[1]), f32)

    def several(i, total):
        for c in range(pieces // loops):
            total = piece(i * (pieces // loops) + c, total)
        return total

    total = lax.fori_loop(0, loops, several, total)
    if not last:
        post(total, weight_n, out_ref)


def ranks_kernel(weight, me_ref, left_ref, right_ref, sig_ref, pre_ref, part_ref, sig_out, *refs):
    pre_outs, sems = refs[:-1], refs[-1]
    slots, _, width = sig_ref.shape
    copies = [
        pltpu.make_async_copy(pre_ref.at[s], o, sems.at[s]) for s, o in enumerate(pre_outs)
    ]
    copies.append(pltpu.make_async_copy(sig_ref, sig_out, sems.at[slots]))
    for copy in copies:
        copy.start()
    g = k = None
    for s in range(slots):
        at = pl.ds(pl.multiple_of((me_ref[0] ^ s) * width, width), width)
        a = dot(pre_ref[s], right_ref[at, :], NN)
        b = dot(sig_ref[s], left_ref[s * width : (s + 1) * width, :], NN)
        g, k = (a, b) if g is None else (g + a, k + b)
    chunk = part_ref.shape[1]
    half = g.shape[0] // chunk
    for i in range(half):
        part_ref[i] = (g[i * chunk : (i + 1) * chunk] * weight).astype(bf16)
        part_ref[half + i] = (k[i * chunk : (i + 1) * chunk] * weight).astype(bf16)
    for copy in copies:
        copy.wait()


def again_kernel(in_ref, out_ref):
    total = jnp.sum(in_ref[...].astype(f32), 0).astype(out_ref.dtype)
    for i in range(out_ref.shape[0]):
        out_ref[i] = total


def gradient(weight, slots, me_ref, factor_hbm, ranks, pieces, rows, near, held, sem, sems, use):
    width = rows.shape[0]
    deep = pieces[0].shape[0]
    copies = []
    for s in range(slots):
        at = pl.ds(s * deep, deep)
        for i, (src, dst) in enumerate(((ranks[s], near), (pieces[s], held))):
            copies.append(pltpu.make_async_copy(src, dst.at[at], sems.at[i, s]))
    copies.append(
        pltpu.make_async_copy(
            factor_hbm.at[pl.ds(pl.multiple_of(me_ref[0] * width, width), width)], rows, sem
        )
    )
    for copy in copies:
        copy.start()
    for copy in copies:
        copy.wait()
    size = 4 * block

    def several(i, carry):
        at = pl.ds(pl.multiple_of(i * size, size), size)
        use(at, rows[at].astype(f32) - weight * dot(held[:, at], near[...], TN))
        return carry

    lax.fori_loop(0, width // size, several, 0)


def packing(n):
    return [(o, n - block - o) for o in range(0, n // 2, block)]


def right_kernel(weight, slots, me_ref, factor_hbm, *refs):
    high_hbm, low_hbm, gram_ref = refs[2 * slots : 2 * slots + 3]
    rows, near, held, high, low, sem, sems, out_sem = refs[2 * slots + 3 :]

    def use(at, step):
        high[at], low[at] = halves(step)

    gradient(
        weight, slots, me_ref, factor_hbm, refs[:slots], refs[slots : 2 * slots], rows, near, held, sem, sems, use
    )
    back = [
        pltpu.make_async_copy(v, o, out_sem.at[i])
        for i, (v, o) in enumerate(((high, high_hbm), (low, low_hbm)))
    ]
    for copy in back:
        copy.start()
    n = high.shape[1]
    for group in packing(n):
        packed = jnp.concatenate(
            [
                dot3(
                    (high[:, o : o + block], low[:, o : o + block]), (high[:, o:], low[:, o:]), TN
                )
                for o in group
            ],
            1,
        )
        at = group[0] // 2
        for i in range(block // 2):
            gram_ref[at + i] = packed[2 * i : 2 * i + 2]
    for copy in back:
        copy.wait()


def left_kernel(weight, weight_l, slots, me_ref, high_ref, low_ref, factor_hbm, *refs):
    ranks, signal_hbm, out_ref, (rows, near, held, sem, sems) = (
        refs[:slots], refs[slots], refs[slots + 1], refs[slots + 2 :]
    )
    pieces = [signal_hbm.at[me_ref[0] ^ s] for s in range(slots)]
    upper = high_ref[...], low_ref[...]

    def use(at, step):
        out_ref[at] = (dot3(halves(step), upper, NT) * weight_l).astype(bf16)

    gradient(weight, slots, me_ref, factor_hbm, ranks, pieces, rows, near, held, sem, sems, use)


def diagonal(rows):
    groups = len(rows)
    wide = (8, block)
    lane = lax.broadcasted_iota(jnp.int32, wide, 1)
    sub = lax.broadcasted_iota(jnp.int32, wide, 0)
    rows = list(rows)
    ones = [jnp.where(lane == sub + 8 * g, 1.0, 0.0).astype(f32) for g in range(groups)]
    for g in range(groups):
        cols = [jnp.broadcast_to(rows[g][:, 8 * g + k : 8 * g + k + 1], wide) for k in range(8)]
        pivots = []
        a, e, root = rows[g], ones[g], None
        for j in range(8):
            d = jnp.broadcast_to(cols[j][j : j + 1, :], wide)
            inverse = 1.0 / d
            col = jnp.where(sub > j, cols[j], 0.0)
            us = [None] * 8
            for k in range(j + 1, 8):
                us[k] = jnp.broadcast_to(cols[k][j : j + 1, :], wide)
                cols[k] = cols[k] - (col * us[k]) * inverse
            ua = jnp.broadcast_to(a[j : j + 1, :], wide)
            ue = jnp.broadcast_to(e[j : j + 1, :], wide)
            m = col * inverse
            a = a - m * ua
            e = e - m * ue
            r = lax.rsqrt(d)
            root = r if root is None else jnp.where(sub == j, r, root)
            pivots.append((inverse, us, ua, ue))
        ones[g] = e * root
        for h in range(g + 1, groups):
            cols = [jnp.broadcast_to(rows[h][:, 8 * g + k : 8 * g + k + 1], wide) for k in range(8)]
            a, e = rows[h], ones[h]
            for j in range(8):
                inverse, us, ua, ue = pivots[j]
                m = cols[j] * inverse
                for k in range(j + 1, 8):
                    cols[k] = cols[k] - m * us[k]
                a = a - m * ua
                e = e - m * ue
            rows[h], ones[h] = a, e
    return ones


def finish_kernel(weight_r, gram_ref, rh, rl, upper_hi, upper_lo, right_ref, aug, part, steps, sems):
    n = right_ref.shape[1]
    blocks = n // block
    copies = [pltpu.make_async_copy(v, steps.at[i], sems.at[i]) for i, v in enumerate((rh, rl))]
    for copy in copies:
        copy.start()
    row = lax.broadcasted_iota(jnp.int32, (n, n), 0)
    col = lax.broadcasted_iota(jnp.int32, (n, n), 1)
    for group in packing(n):
        for i in range(block // 2):
            pair, at = gram_ref[group[0] // 2 + i], 0
            for o in group:
                aug[o + 2 * i : o + 2 * i + 2, o:n] = pair[:, at : at + n - o]
                at += n - o
    aug[:, n:] = jnp.where(row == col, 1.0, 0.0).astype(f32)

    def panel(p, carry):
        o = pl.multiple_of(p * block, block)
        ones = diagonal(
            [
                aug[pl.ds(pl.multiple_of(o + 8 * g, 8), 8), pl.ds(o, block)]
                for g in range(block // 8)
            ]
        )
        for g in range(block // 8):
            part[8 * g : 8 * g + 8, :] = ones[g]
        for k in range(blocks):

            @pl.when(p == k)
            def _(k=k):
                lo = k * block
                new = dot(part[...], aug[lo : lo + block, lo : n + lo + block], NN, highest)
                aug[lo : lo + block, lo : n + lo + block] = new
                if k + 1 < blocks:
                    aug[lo + block :, lo + block : n + lo + block] -= dot(
                        new[:, block : n - lo], new[:, block:], TN, highest
                    )

        return carry

    lax.fori_loop(0, blocks, panel, 0)
    upper_hi[...], upper_lo[...] = halves(jnp.where(row <= col, aug[:, :n], 0.0))
    inverse = halves(jnp.where(row >= col, aug[:, n:], 0.0))
    for copy in copies:
        copy.wait()
    right_ref[...] = (dot3((steps[0], steps[1]), inverse, NT) * weight_r).astype(bf16)


def call(kernel, args, outs, name, limit, scratch=(), aliases=None, far=(), far_outs=(), flops=None):
    hbm = pl.BlockSpec(memory_space=pltpu.HBM)
    smem = pl.BlockSpec(memory_space=pltpu.SMEM)
    args = [
        pltpu.with_memory_space_constraint(a, pltpu.HBM) if i in far else a
        for i, a in enumerate(args)
    ]
    outs = [
        pltpu.HBM(o.shape, o.dtype) if i in far_outs else o for i, o in enumerate(outs)
    ]
    return pl.pallas_call(
        kernel,
        out_shape=outs,
        in_specs=[
            smem if a.dtype == jnp.int32 else hbm if i in far else vmem for i, a in enumerate(args)
        ],
        out_specs=[hbm if i in far_outs else vmem for i in range(len(outs))],
        scratch_shapes=scratch,
        input_output_aliases=aliases or {},
        name=name,
        cost_estimate=flops and pl.CostEstimate(flops=flops, transcendentals=0, bytes_accessed=0),
        compiler_params=pltpu.CompilerParams(vmem_limit_bytes=limit << 20),
    )(*args)


def shards(
    drive,
    learning,
    membrane_init,
    adapt_init,
    trace_init,
    membrane_decay,
    adapt_decay,
    adapt_gain,
    threshold,
    left_factor,
    right_factor,
):
    local_neurons, rank_width = left_factor.shape
    step_count, local_trials = drive.shape[:2]
    neuron_shards = lax.axis_size("neuron")
    trial_shards = lax.axis_size("trial")
    neuron_count = local_neurons * neuron_shards
    norm_neurons = 1.0 / math.sqrt(neuron_count)
    norm_rank = 1.0 / math.sqrt(rank_width)
    stored = local_neurons // trial_shards
    struct = jax.ShapeDtypeStruct
    decay, adecay, gain, level = (
        v.reshape(1, -1) for v in (membrane_decay, adapt_decay, adapt_gain, threshold)
    )
    state = pltpu.VMEM(membrane_init.shape, f32)
    sent = struct((neuron_shards, local_trials, rank_width), bf16)
    rows = step_count * local_trials
    slots = trial_shards
    everyone = ("neuron", "trial")
    me = lax.axis_index("trial").astype(jnp.int32).reshape(1)
    copy_sem = pltpu.SemaphoreType.DMA

    spikes, out, right_near, drive_near, learn_near = call(
        lambda *r: start_kernel(norm_neurons, *r),
        (me, gain, level, membrane_init, adapt_init, right_factor, drive, learning),
        [
            state,
            sent,
            pltpu.VMEM(right_factor.shape, bf16),
            pltpu.VMEM(drive.shape, bf16),
            pltpu.VMEM(learning.shape, bf16),
        ],
        "start",
        8,
        (
            pltpu.VMEM(gain.shape, f32),
            pltpu.VMEM(level.shape, f32),
            pltpu.VMEM(membrane_init.shape, f32),
            pltpu.VMEM(adapt_init.shape, f32),
            copy_sem((8,)),
            copy_sem((6,)),
        ),
        far=tuple(range(1, 8)),
    )
    states = [membrane_init, adapt_init, trace_init, spikes]
    kept = pltpu.VMEM((slots, rows, stored), bf16)
    left_near = left_factor
    every = ()

    def exchange(values, k):
        return lax.ppermute(values, "trial", [(i, i ^ k) for i in range(slots)]) if k else values

    for moment in range(step_count):
        first, last = moment == 0, moment + 1 == step_count
        got = swap(out, "neuron")
        result = call(
            lambda *r, moment=moment: step_kernel(norm_neurons, norm_rank, moment, step_count, *r),
            (me, got, decay, adecay, gain, level, drive_near, learn_near, *states, left_near, right_near, *every),
            [kept, kept]
            + ([] if last else [state, state, state, state, sent])
            + ([pltpu.VMEM(left_factor.shape, bf16)] if first else []),
            "step",
            8,
            (copy_sem((slots,)),) if first else (),
            {} if first else {14: 0, 15: 1} | ({} if last else {8 + i: 2 + i for i in range(4)}),
            (12,) if first else (),
        )
        every = result[:2]
        if not last:
            states, out = result[2:6], result[6]
        if first:
            left_near = result[7]

    chunk = 2 * rows // neuron_shards
    slot = struct((rows, stored), bf16)
    part, signal_all, *presyn_mine = call(
        lambda *r: ranks_kernel(norm_neurons, *r),
        (me, left_near, right_near, *every),
        [struct((neuron_shards, chunk, rank_width), bf16), struct((slots, rows, stored), bf16)]
        + [slot] * slots,
        "ranks",
        16,
        (copy_sem((slots + 1,)),),
        far_outs=tuple(range(1, 2 + slots)),
    )
    down = [(i, (i - 2) % slots) for i in range(slots)]
    over = [(i, ((i - 2) % slots) ^ 1) for i in range(slots)]
    opposite = {4: exchange(presyn_mine[4], 4), 5: lax.ppermute(presyn_mine[5], "trial", down)}
    presyn_mine = [opposite[k] if k in opposite else exchange(v, k) for k, v in enumerate(presyn_mine)]

    def again(blocks, copies):
        return call(
            again_kernel,
            (blocks,),
            [struct((copies,) + blocks.shape[1:], blocks.dtype)],
            "again",
            8,
        )[0]

    def everywhere(values):
        same = [exchange(values, 2 * j) for j in range(slots // 2)]
        return [v for s in same for v in (s, exchange(s, 1))]

    mine = again(swap(part, "neuron"), neuron_shards)
    near = [4, 5, 2, 3, 6]
    mine, *moved = lax.optimization_barrier((mine, *[presyn_mine[k] for k in near]))
    for k, v in zip(near, moved, strict=True):
        presyn_mine[k] = v
    presyn_mine[5] = lax.ppermute(presyn_mine[5], "trial", over)
    ranks = swap(mine, "neuron")
    ranks = ranks.reshape(2, rows, rank_width)
    pair = struct((stored, rank_width), bf16)
    blocks = struct((rank_width // 4, 2, rank_width + block), f32)
    weight = learn_rate * norm_rank

    far = 2 * slots + 1
    scratch = (
        pltpu.VMEM((stored, rank_width), bf16),
        pltpu.VMEM((slots * rows, rank_width), bf16),
        pltpu.VMEM((slots * rows, stored), bf16),
    )
    sems = (copy_sem, copy_sem((2, slots)))
    right_hi, right_lo, gram_part = call(
        lambda *r: right_kernel(weight, slots, *r),
        (me, right_factor, *everywhere(ranks[1]), *presyn_mine),
        [pair, pair, blocks],
        "right",
        32,
        (*scratch, *scratch[:1], *scratch[:1], *sems, copy_sem((2,))),
        far=tuple(range(1, 1 + far)),
        far_outs=(0, 1),
    )
    gram_part, rank_g = lax.optimization_barrier((gram_part, ranks[0]))
    rank_g = everywhere(rank_g)
    gram_one = swap(again(swap(gram_part, everyone), neuron_shards * slots), everyone)
    gram_one, signal_all = lax.optimization_barrier((gram_one, signal_all))
    signal_mine = swap(signal_all, "trial")
    square = struct((rank_width, rank_width), bf16)
    upper_hi, upper_lo, right_new = call(
        lambda *r: finish_kernel(math.sqrt(neuron_count), *r),
        (gram_one, right_hi, right_lo),
        [square, square, pair],
        "finish",
        24,
        (
            pltpu.VMEM((rank_width, 2 * rank_width), f32),
            pltpu.VMEM((block, block), f32),
            pltpu.VMEM((2, stored, rank_width), bf16),
            copy_sem((2,)),
        ),
        far=(1, 2),
        flops=20 * 10**9,
    )
    (left_new,) = call(
        lambda *r: left_kernel(weight, norm_neurons, slots, *r),
        (me, upper_hi, upper_lo, left_factor, *rank_g, signal_mine),
        [pair],
        "left",
        32,
        (*scratch, *sems),
        far=tuple(range(3, 5 + slots)),
    )
    return (left_new, right_new)


def solution(mesh):
    in_specs = (
        P(None, "trial", "neuron"),
        P(None, "trial", "neuron"),
        P("trial", "neuron"),
        P("trial", "neuron"),
        P("trial", "neuron"),
        P("neuron"),
        P("neuron"),
        P("neuron"),
        P("neuron"),
        P("neuron", None),
        P("neuron", None),
    )
    out_specs = (P(("neuron", "trial"), None), P(("neuron", "trial"), None))
    return jax.shard_map(shards, mesh=mesh, in_specs=in_specs, out_specs=out_specs, check_vma=False)
```

profile of v0, /device:TPU:1, one launch (start us, length us, event | category | flops | bytes accessed | tf_op | source)
XLA Modules:
  0.0 275.9 jit_solution(10689921654174016682)
XLA Ops:
  0.7 5.4 %start.1 = (f32[16,8192]{1,0:T(8,128)S(1)}, bf16[16,16,512]{2,1,0:T(8,128)(2,1)S(1)}, bf16[8192,512]{1,0:T(8,128)(2,1)S(1)}, bf16[8,16,8192]{2,1,0:T(8,128)(2,1)S(1)}, bf16[8,16,8192]{2,1,0:T(8,128)(2,1)S(1)}) custom-call(s32[1]{0:T(128)} %bitcast.r_0_, f32[1,8192]{1,0:T(1,128)} %bitcast.7, f32[1,8192]{1,0:T(1,128)} %bitcast.16, f32[16,8192]{1,0:T(8,128)} %r_8_.1, ...), custom_call_target="tpu_custom_call" | custom-call | tf_op jit(solution)/shard_map/start/pallas_call | solution.py:368
  6.1 15.9 %all_to_all.65.r_1_ = bf16[16,16,512]{2,1,0:T(8,128)(2,1)S(1)} all-to-all(bf16[16,16,512]{2,1,0:T(8,128)(2,1)S(1)} %get-tuple-element.85), channel_id=1, replica_groups=mesh['neuron'=16,'trial'=8] {'neuron'}, dimensions={0} | all-to-all | bytes 524288 | tf_op jit(solution)/shard_map/all_to_all | solution.py:31
  22.1 5.1 %step.8 = (bf16[8,128,1024]{2,1,0:T(8,128)(2,1)S(1)}, bf16[8,128,1024]{2,1,0:T(8,128)(2,1)S(1)}, f32[16,8192]{1,0:T(8,128)S(1)}, f32[16,8192]{1,0:T(8,128)S(1)},...) custom-call(s32[1]{0:T(128)} %bitcast.r_0_, ...), custom_call_target="tpu_custom_call" | custom-call | tf_op jit(solution)/shard_map/step/pallas_call | solution.py:368
  27.2 10.5 %all_to_all.66.r_1_ = bf16[16,16,512]{2,1,0:T(8,128)(2,1)S(1)} all-to-all(bf16[16,16,512]{2,1,0:T(8,128)(2,1)S(1)} %get-tuple-element.91), channel_id=1, replica_groups=mesh['neuron'=16,'trial'=8] {'neuron'}, dimensions={0} | all-to-all | bytes 524288 | tf_op jit(solution)/shard_map/all_to_all | solution.py:31
  37.7 3.9 %step.9 = (bf16[8,128,1024]{2,1,0:T(8,128)(2,1)S(1)}, bf16[8,128,1024]{2,1,0:T(8,128)(2,1)S(1)}, f32[16,8192]{1,0:T(8,128)S(1)}, f32[16,8192]{1,0:T(8,128)S(1)},...) custom-call(s32[1]{0:T(128)} %bitcast.r_0_, ...), custom_call_target="tpu_custom_call", output_to_operand_aliasing={{0}: (14, {}), {1}: (15, {}), {2}: (8, {}), {3}: (9, {}), {... | custom-call | tf_op jit(solution)/shard_map/step/pallas_call | solution.py:368
  41.6 10.5 %all_to_all.67.r_1_ = bf16[16,16,512]{2,1,0:T(8,128)(2,1)S(1)} all-to-all(bf16[16,16,512]{2,1,0:T(8,128)(2,1)S(1)} %get-tuple-element.98), channel_id=1, replica_groups=mesh['neuron'=16,'trial'=8] {'neuron'}, dimensions={0} | all-to-all | bytes 524288 | tf_op jit(solution)/shard_map/all_to_all | solution.py:31
  55.9 10.2 %all_to_all.68.r_1_ = bf16[16,16,512]{2,1,0:T(8,128)(2,1)S(1)} all-to-all(bf16[16,16,512]{2,1,0:T(8,128)(2,1)S(1)} %get-tuple-element.105), channel_id=1, replica_groups=mesh['neuron'=16,'trial'=8] {'neuron'}, dimensions={0} | all-to-all | bytes 524288 | tf_op jit(solution)/shard_map/all_to_all | solution.py:31
  69.9 10.2 %all_to_all.69.r_1_ = bf16[16,16,512]{2,1,0:T(8,128)(2,1)S(1)} all-to-all(bf16[16,16,512]{2,1,0:T(8,128)(2,1)S(1)} %get-tuple-element.112), channel_id=1, replica_groups=mesh['neuron'=16,'trial'=8] {'neuron'}, dimensions={0} | all-to-all | bytes 524288 | tf_op jit(solution)/shard_map/all_to_all | solution.py:31
  84.0 10.2 %all_to_all.70.r_1_ = bf16[16,16,512]{2,1,0:T(8,128)(2,1)S(1)} all-to-all(bf16[16,16,512]{2,1,0:T(8,128)(2,1)S(1)} %get-tuple-element.119), channel_id=1, replica_groups=mesh['neuron'=16,'trial'=8] {'neuron'}, dimensions={0} | all-to-all | bytes 524288 | tf_op jit(solution)/shard_map/all_to_all | solution.py:31
  98.0 10.2 %all_to_all.71.r_1_ = bf16[16,16,512]{2,1,0:T(8,128)(2,1)S(1)} all-to-all(bf16[16,16,512]{2,1,0:T(8,128)(2,1)S(1)} %get-tuple-element.126), channel_id=1, replica_groups=mesh['neuron'=16,'trial'=8] {'neuron'}, dimensions={0} | all-to-all | bytes 524288 | tf_op jit(solution)/shard_map/all_to_all | solution.py:31
  112.0 10.2 %all_to_all.72.r_1_ = bf16[16,16,512]{2,1,0:T(8,128)(2,1)S(1)} all-to-all(bf16[16,16,512]{2,1,0:T(8,128)(2,1)S(1)} %get-tuple-element.133), channel_id=1, replica_groups=mesh['neuron'=16,'trial'=8] {'neuron'}, dimensions={0} | all-to-all | bytes 524288 | tf_op jit(solution)/shard_map/all_to_all | solution.py:31
  124.7 3.9 %ranks.1 = (bf16[16,16,512]{2,1,0:T(8,128)(2,1)S(1)}, bf16[8,128,1024]{2,1,0:T(8,128)(2,1)}, bf16[128,1024]{1,0:T(8,128)(2,1)}, bf16[128,1024]{1,0:T(8,128)(2,1)...) custom-call(s32[1]{0:T(128)} %bitcast.r_0_, ...), custom_call_target="tpu_custom_call" | custom-call | tf_op jit(solution)/shard_map/ranks/pallas_call | solution.py:368
  132.9 13.1 %collective-permute-start.3 = (bf16[128,1024]{1,0:T(8,128)(2,1)}, bf16[128,1024]{1,0:T(8,128)(2,1)S(1)}, u32[]{:S(2)}, u32[]{:S(2)}) collective-permute-start(bf16[128,1024]{1,0:T(8,128)(2,1)} %get-tuple-element.146), channel_id=1, source_target_pairs={{0,3},{1,2},{2,1},{3,0},{4,7},{5,6},{6,5},{7,4},{8,11},{9,10},{10,... | collective-permute-start | bytes 786440 | tf_op jit(solution)/shard_map/ppermute | solution.py:444
  146.0 10.6 %all_to_all.73.in_ref = bf16[16,16,512]{2,1,0:T(8,128)(2,1)S(1)} all-to-all(bf16[16,16,512]{2,1,0:T(8,128)(2,1)S(1)} %get-tuple-element.142), channel_id=1, replica_groups=mesh['neuron'=16,'trial'=8] {'neuron'}, dimensions={0} | all-to-all | bytes 524288 | tf_op jit(solution)/shard_map/all_to_all | solution.py:31
  165.4 5.6 %all-to-all-done.9 = bf16[16,16,512]{2,1,0:T(8,128)(2,1)S(1)} async-done(((bf16[16,16,512]{2,1,0:T(8,128)(2,1)}), bf16[16,16,512]{2,1,0:T(8,128)(2,1)S(1)}, u32[]{:S(2)}, u32[]{:S(2)}) %all-to-all-start.9) | async-done | bytes 262176 | tf_op jit(solution)/shard_map/all_to_all | solution.py:31
  182.0 4.2 %collective-permute-done.6.r_4_ = bf16[128,512]{1,0:T(8,128)(2,1)S(1)} collective-permute-done((bf16[128,512]{1,0:T(8,128)(2,1)S(1)}, bf16[128,512]{1,0:T(8,128)(2,1)S(1)}, u32[]{:S(2)}, u32[]{:S(2)}) %collective-permute-start.6) | collective-permute-done | bytes 131104 | tf_op jit(solution)/shard_map/ppermute | solution.py:444
  188.3 5.5 %right.1 = (bf16[1024,512]{1,0:T(8,128)(2,1)}, bf16[1024,512]{1,0:T(8,128)(2,1)}, f32[128,2,640]{2,1,0:T(2,128)S(1)}) custom-call(s32[1]{0:T(128)} %bitcast.r_0_, bf16[8192,512]{1,0:T(8,128)(2,1)} %r_1_.1, bf16[128,512]{1,0:T(8,128)(2,1)} %bitcast.50, bf16[128,512]{1,0:T(8,128)(2,1)} %copy-done.24, bf16[128,512]{1,0:T(8,128)(2,1)} %copy-done.22, ...), custom_call_target="tpu_custom_call" | custom-call | tf_op jit(solution)/shard_map/right/pallas_call | solution.py:368
  193.8 20.1 %all_to_all.74.in_ref = f32[128,2,640]{2,1,0:T(2,128)S(1)} all-to-all(f32[128,2,640]{2,1,0:T(2,128)S(1)} %get-tuple-element.158), channel_id=1, replica_groups=mesh['neuron'=16,'trial'=8] {'neuron','trial'}, dimensions={0} | all-to-all | bytes 1310720 | tf_op jit(solution)/shard_map/all_to_all | solution.py:31
  215.1 4.5 %all-to-all-start.11 = ((f32[128,2,640]{2,1,0:T(2,128)}), f32[128,2,640]{2,1,0:T(2,128)S(1)}, u32[]{:S(2)}, u32[]{:S(2)}) async-start(f32[128,2,640]{2,1,0:T(2,128)} %again.3), calls=%async_computation.11 | async-start | bytes 1310720 | tf_op jit(solution)/shard_map/all_to_all | solution.py:31
  225.0 9.9 %collective-permute-done.20.r_10_ = bf16[128,512]{1,0:T(8,128)(2,1)S(1)} collective-permute-done((bf16[128,512]{1,0:T(8,128)(2,1)S(1)}, bf16[128,512]{1,0:T(8,128)(2,1)S(1)}, u32[]{:S(2)}, u32[]{:S(2)}) %collective-permute-start.20) | collective-permute-done | bytes 131104 | tf_op jit(solution)/shard_map/ppermute | solution.py:444
  236.5 6.1 %all-to-all-start.12 = ((bf16[8,128,1024]{2,1,0:T(8,128)(2,1)}), bf16[8,128,1024]{2,1,0:T(8,128)(2,1)}, u32[]{:S(2)}, u32[]{:S(2)}) async-start(bf16[8,128,1024]{2,1,0:T(8,128)(2,1)} %get-tuple-element.166), calls=%async_computation.12 | async-start | bytes 4194304 | tf_op jit(solution)/shard_map/all_to_all | solution.py:31
  242.7 21.6 %finish.1 = (bf16[512,512]{1,0:T(8,128)(2,1)S(1)}, bf16[512,512]{1,0:T(8,128)(2,1)S(1)}, bf16[1024,512]{1,0:T(8,128)(2,1)}) custom-call(f32[128,2,640]{2,1,0:T(2,128)S(1)} %all-to-all-done.11.r_0_, bf16[1024,512]{1,0:T(8,128)(2,1)} %get-tuple-element.161.r_1_, bf16[1024,512]{1,0:T(8,128)(2,1)} %get-tuple-element.162.r_2_), custom_call_target="tpu_custom_call" | custom-call | flops 20000000000 | tf_op jit(solution)/shard_map/finish/pallas_call | solution.py:368
  264.3 4.8 %all-to-all-done.12.r_12_ = bf16[8,128,1024]{2,1,0:T(8,128)(2,1)} async-done(((bf16[8,128,1024]{2,1,0:T(8,128)(2,1)}), bf16[8,128,1024]{2,1,0:T(8,128)(2,1)}, u32[]{:S(2)}, u32[]{:S(2)}) %all-to-all-start.12) | async-done | bytes 2097184 | tf_op jit(solution)/shard_map/all_to_all | solution.py:31
  269.2 6.6 %left.1 = bf16[1024,512]{1,0:T(8,128)(2,1)} custom-call(s32[1]{0:T(128)} %bitcast.r_0_, bf16[512,512]{1,0:T(8,128)(2,1)S(1)} %get-tuple-element.163.r_1_, bf16[512,512]{1,0:T(8,128)(2,1)S(1)} %get-tuple-element.164.r_2_, bf16[8192,512]{1,0:T(8,128)(2,1)} %r_3_.3, bf16[128,512]{1,0:T(8,128)(2,1)} %bitcast.45, bf16[128,512]{1,0:T(8,128)(2,1)} %copy-done.21, ...), custom_call_target="tpu_custom_call" | custom-call | tf_op jit(solution)/shard_map/left/pallas_call | solution.py:368
  (112 shorter events, 56.0 us)
Async XLA Ops:
  128.6 28.8 %collective-permute-start = (bf16[128,1024]{1,0:T(8,128)(2,1)}, bf16[128,1024]{1,0:T(8,128)(2,1)S(1)}, u32[]{:S(2)}, u32[]{:S(2)}) collective-permute-start(bf16[128,1024]{1,0:T(8,128)(2,1)} %get-tuple-element.143), channel_id=1, source_target_pairs={{0,4},{1,5},{2,6},{3,7},{4,0},{5,1},{6,2},{7,3},{8,12},{9,13},{10,... | collective-permute-start | bytes 786440 | tf_op jit(solution)/shard_map/ppermute | solution.py:444
  131.4 26.0 %collective-permute-start.1 = (bf16[128,1024]{1,0:T(8,128)(2,1)}, bf16[128,1024]{1,0:T(8,128)(2,1)S(1)}, u32[]{:S(2)}, u32[]{:S(2)}) collective-permute-start(bf16[128,1024]{1,0:T(8,128)(2,1)} %get-tuple-element.144), channel_id=1, source_target_pairs={{0,6},{1,7},{2,0},{3,1},{4,2},{5,3},{6,4},{7,5},{8,14},{9,15},{10,... | collective-permute-start | bytes 786440 | tf_op jit(solution)/shard_map/ppermute | solution.py:481
  132.3 25.1 %collective-permute-start.2 = (bf16[128,1024]{1,0:T(8,128)(2,1)}, bf16[128,1024]{1,0:T(8,128)(2,1)S(1)}, u32[]{:S(2)}, u32[]{:S(2)}) collective-permute-start(bf16[128,1024]{1,0:T(8,128)(2,1)} %get-tuple-element.145), channel_id=1, source_target_pairs={{0,2},{1,3},{2,0},{3,1},{4,6},{5,7},{6,4},{7,5},{8,10},{9,11},{10,... | collective-permute-start | bytes 786440 | tf_op jit(solution)/shard_map/ppermute | solution.py:444
  132.9 26.0 %collective-permute-start.3 = (bf16[128,1024]{1,0:T(8,128)(2,1)}, bf16[128,1024]{1,0:T(8,128)(2,1)S(1)}, u32[]{:S(2)}, u32[]{:S(2)}) collective-permute-start(bf16[128,1024]{1,0:T(8,128)(2,1)} %get-tuple-element.146), channel_id=1, source_target_pairs={{0,3},{1,2},{2,1},{3,0},{4,7},{5,6},{6,5},{7,4},{8,11},{9,10},{10,... | collective-permute-start | bytes 786440 | tf_op jit(solution)/shard_map/ppermute | solution.py:444
  146.0 12.9 %collective-permute-start.4 = (bf16[128,1024]{1,0:T(8,128)(2,1)}, bf16[128,1024]{1,0:T(8,128)(2,1)S(1)}, u32[]{:S(2)}, u32[]{:S(2)}) collective-permute-start(bf16[128,1024]{1,0:T(8,128)(2,1)} %get-tuple-element.147), channel_id=1, source_target_pairs={{0,6},{1,7},{2,4},{3,5},{4,2},{5,3},{6,0},{7,1},{8,14},{9,15},{10,... | collective-permute-start | bytes 786440 | tf_op jit(solution)/shard_map/ppermute | solution.py:444
  159.0 12.0 %all-to-all-start.9 = ((bf16[16,16,512]{2,1,0:T(8,128)(2,1)}), bf16[16,16,512]{2,1,0:T(8,128)(2,1)S(1)}, u32[]{:S(2)}, u32[]{:S(2)}) async-start(bf16[16,16,512]{2,1,0:T(8,128)(2,1)} %again.2), calls=%async_computation.9 | async-start | bytes 524288 | tf_op jit(solution)/shard_map/all_to_all | solution.py:31
  162.5 13.1 %collective-permute-start.12 = (bf16[128,1024]{1,0:T(8,128)(2,1)}, bf16[128,1024]{1,0:T(8,128)(2,1)S(1)}, u32[]{:S(2)}, u32[]{:S(2)}) collective-permute-start(bf16[128,1024]{1,0:T(8,128)(2,1)} %get-tuple-element.150), channel_id=1, source_target_pairs={{0,1},{1,0},{2,3},{3,2},{4,5},{5,4},{6,7},{7,6},{8,9},{9,8},{10,11... | collective-permute-start | bytes 786440 | tf_op jit(solution)/shard_map/ppermute | solution.py:444
  162.7 13.1 %collective-permute-start.14 = (bf16[128,1024]{1,0:T(8,128)(2,1)}, bf16[128,1024]{1,0:T(8,128)(2,1)S(1)}, u32[]{:S(2)}, u32[]{:S(2)}) collective-permute-start(bf16[128,1024]{1,0:T(8,128)(2,1)} %get-tuple-element.156), channel_id=1, source_target_pairs={{0,7},{1,6},{2,5},{3,4},{4,3},{5,2},{6,1},{7,0},{8,15},{9,14},{10,... | collective-permute-start | bytes 786440 | tf_op jit(solution)/shard_map/ppermute | solution.py:444
  171.0 5.3 %collective-permute-start.10 = (bf16[128,512]{1,0:T(8,128)(2,1)S(1)}, bf16[128,512]{1,0:T(8,128)(2,1)S(1)}, u32[]{:S(2)}, u32[]{:S(2)}) collective-permute-start(bf16[128,512]{1,0:T(8,128)(2,1)S(1)} %bitcast.46), channel_id=1, source_target_pairs={{0,6},{1,7},{2,4},{3,5},{4,2},{5,3},{6,0},{7,1},{8,14},{9,15},{10,... | collective-permute-start | bytes 393224 | tf_op jit(solution)/shard_map/ppermute | solution.py:444
  172.0 14.3 %collective-permute-start.13 = (bf16[128,1024]{1,0:T(8,128)(2,1)S(1)}, bf16[128,1024]{1,0:T(8,128)(2,1)S(1)}, u32[]{:S(2)}, u32[]{:S(2)}) collective-permute-start(bf16[128,1024]{1,0:T(8,128)(2,1)S(1)} %collective-permute-done.1), channel_id=1, source_target_pairs={{0,7},{1,6},{2,1},{3,0},{4,3},{5,2},{6,5},{7,4},{8,15},{9,14},{10,... | collective-permute-start | bytes 786440 | tf_op jit(solution)/shard_map/ppermute | solution.py:502
  175.1 6.7 %collective-permute-start.8 = (bf16[128,512]{1,0:T(8,128)(2,1)S(1)}, bf16[128,512]{1,0:T(8,128)(2,1)S(1)}, u32[]{:S(2)}, u32[]{:S(2)}) collective-permute-start(bf16[128,512]{1,0:T(8,128)(2,1)S(1)} %bitcast.47), channel_id=1, source_target_pairs={{0,4},{1,5},{2,6},{3,7},{4,0},{5,1},{6,2},{7,3},{8,12},{9,13},{10,... | collective-permute-start | bytes 393224 | tf_op jit(solution)/shard_map/ppermute | solution.py:444
  175.6 10.7 %collective-permute-start.6 = (bf16[128,512]{1,0:T(8,128)(2,1)S(1)}, bf16[128,512]{1,0:T(8,128)(2,1)S(1)}, u32[]{:S(2)}, u32[]{:S(2)}) collective-permute-start(bf16[128,512]{1,0:T(8,128)(2,1)S(1)} %bitcast.48), channel_id=1, source_target_pairs={{0,2},{1,3},{2,0},{3,1},{4,6},{5,7},{6,4},{7,5},{8,10},{9,11},{10,... | collective-permute-start | bytes 393224 | tf_op jit(solution)/shard_map/ppermute | solution.py:444
  175.8 10.5 %collective-permute-start.5 = (bf16[128,512]{1,0:T(8,128)(2,1)S(1)}, bf16[128,512]{1,0:T(8,128)(2,1)S(1)}, u32[]{:S(2)}, u32[]{:S(2)}) collective-permute-start(bf16[128,512]{1,0:T(8,128)(2,1)S(1)} %bitcast.49), channel_id=1, source_target_pairs={{0,1},{1,0},{2,3},{3,2},{4,5},{5,4},{6,7},{7,6},{8,9},{9,8},{10,11... | collective-permute-start | bytes 393224 | tf_op jit(solution)/shard_map/ppermute | solution.py:444
  176.4 10.0 %collective-permute-start.11 = (bf16[128,512]{1,0:T(8,128)(2,1)S(1)}, bf16[128,512]{1,0:T(8,128)(2,1)S(1)}, u32[]{:S(2)}, u32[]{:S(2)}) collective-permute-start(bf16[128,512]{1,0:T(8,128)(2,1)S(1)} %collective-permute-done.10.r_8_), channel_id=1, source_target_pairs={{0,1},{1,0},{2,3},{3,2},{4,5},{5,4},{6,7},{7,6},{8,9},{9,8},{10,11... | collective-permute-start | bytes 393224 | tf_op jit(solution)/shard_map/ppermute | solution.py:444
  181.8 4.5 %collective-permute-start.9 = (bf16[128,512]{1,0:T(8,128)(2,1)S(1)}, bf16[128,512]{1,0:T(8,128)(2,1)S(1)}, u32[]{:S(2)}, u32[]{:S(2)}) collective-permute-start(bf16[128,512]{1,0:T(8,128)(2,1)S(1)} %collective-permute-done.8.r_6_), channel_id=1, source_target_pairs={{0,1},{1,0},{2,3},{3,2},{4,5},{5,4},{6,7},{7,6},{8,9},{9,8},{10,11... | collective-permute-start | bytes 393224 | tf_op jit(solution)/shard_map/ppermute | solution.py:444
  215.1 21.2 %all-to-all-start.11 = ((f32[128,2,640]{2,1,0:T(2,128)}), f32[128,2,640]{2,1,0:T(2,128)S(1)}, u32[]{:S(2)}, u32[]{:S(2)}) async-start(f32[128,2,640]{2,1,0:T(2,128)} %again.3), calls=%async_computation.11 | async-start | bytes 1310720 | tf_op jit(solution)/shard_map/all_to_all | solution.py:31
  219.6 15.4 %collective-permute-start.20 = (bf16[128,512]{1,0:T(8,128)(2,1)S(1)}, bf16[128,512]{1,0:T(8,128)(2,1)S(1)}, u32[]{:S(2)}, u32[]{:S(2)}) collective-permute-start(bf16[128,512]{1,0:T(8,128)(2,1)S(1)} %bitcast.41), channel_id=1, source_target_pairs={{0,6},{1,7},{2,4},{3,5},{4,2},{5,3},{6,0},{7,1},{8,14},{9,15},{10,... | collective-permute-start | bytes 393224 | tf_op jit(solution)/shard_map/ppermute | solution.py:444
  222.5 13.3 %collective-permute-start.18 = (bf16[128,512]{1,0:T(8,128)(2,1)S(1)}, bf16[128,512]{1,0:T(8,128)(2,1)S(1)}, u32[]{:S(2)}, u32[]{:S(2)}) collective-permute-start(bf16[128,512]{1,0:T(8,128)(2,1)S(1)} %bitcast.42), channel_id=1, source_target_pairs={{0,4},{1,5},{2,6},{3,7},{4,0},{5,1},{6,2},{7,3},{8,12},{9,13},{10,... | collective-permute-start | bytes 393224 | tf_op jit(solution)/shard_map/ppermute | solution.py:444
  223.1 12.8 %collective-permute-start.16 = (bf16[128,512]{1,0:T(8,128)(2,1)S(1)}, bf16[128,512]{1,0:T(8,128)(2,1)S(1)}, u32[]{:S(2)}, u32[]{:S(2)}) collective-permute-start(bf16[128,512]{1,0:T(8,128)(2,1)S(1)} %bitcast.43), channel_id=1, source_target_pairs={{0,2},{1,3},{2,0},{3,1},{4,6},{5,7},{6,4},{7,5},{8,10},{9,11},{10,... | collective-permute-start | bytes 393224 | tf_op jit(solution)/shard_map/ppermute | solution.py:444
  223.2 41.1 %collective-permute-start.15 = (bf16[128,512]{1,0:T(8,128)(2,1)S(1)}, bf16[128,512]{1,0:T(8,128)(2,1)S(1)}, u32[]{:S(2)}, u32[]{:S(2)}) collective-permute-start(bf16[128,512]{1,0:T(8,128)(2,1)S(1)} %bitcast.44), channel_id=1, source_target_pairs={{0,1},{1,0},{2,3},{3,2},{4,5},{5,4},{6,7},{7,6},{8,9},{9,8},{10,11... | collective-permute-start | bytes 393224 | tf_op jit(solution)/shard_map/ppermute | solution.py:444
  235.0 29.3 %collective-permute-start.21 = (bf16[128,512]{1,0:T(8,128)(2,1)S(1)}, bf16[128,512]{1,0:T(8,128)(2,1)S(1)}, u32[]{:S(2)}, u32[]{:S(2)}) collective-permute-start(bf16[128,512]{1,0:T(8,128)(2,1)S(1)} %collective-permute-done.20.r_10_), channel_id=1, source_target_pairs={{0,1},{1,0},{2,3},{3,2},{4,5},{5,4},{6,7},{7,6},{8,9},{9,8},{10,11... | collective-permute-start | bytes 393224 | tf_op jit(solution)/shard_map/ppermute | solution.py:444
  235.8 28.5 %collective-permute-start.19 = (bf16[128,512]{1,0:T(8,128)(2,1)S(1)}, bf16[128,512]{1,0:T(8,128)(2,1)S(1)}, u32[]{:S(2)}, u32[]{:S(2)}) collective-permute-start(bf16[128,512]{1,0:T(8,128)(2,1)S(1)} %collective-permute-done.18.r_8_), channel_id=1, source_target_pairs={{0,1},{1,0},{2,3},{3,2},{4,5},{5,4},{6,7},{7,6},{8,9},{9,8},{10,11... | collective-permute-start | bytes 393224 | tf_op jit(solution)/shard_map/ppermute | solution.py:444
  235.9 28.4 %collective-permute-start.17 = (bf16[128,512]{1,0:T(8,128)(2,1)S(1)}, bf16[128,512]{1,0:T(8,128)(2,1)S(1)}, u32[]{:S(2)}, u32[]{:S(2)}) collective-permute-start(bf16[128,512]{1,0:T(8,128)(2,1)S(1)} %collective-permute-done.16.r_6_), channel_id=1, source_target_pairs={{0,1},{1,0},{2,3},{3,2},{4,5},{5,4},{6,7},{7,6},{8,9},{9,8},{10,11... | collective-permute-start | bytes 393224 | tf_op jit(solution)/shard_map/ppermute | solution.py:444
  236.5 32.6 %all-to-all-start.12 = ((bf16[8,128,1024]{2,1,0:T(8,128)(2,1)}), bf16[8,128,1024]{2,1,0:T(8,128)(2,1)}, u32[]{:S(2)}, u32[]{:S(2)}) async-start(bf16[8,128,1024]{2,1,0:T(8,128)(2,1)} %get-tuple-element.166), calls=%async_computation.12 | async-start | bytes 4194304 | tf_op jit(solution)/shard_map/all_to_all | solution.py:31
  (31 other events, 408.6 us)
where the time goes:
time: 277 us; the launch traced here: 276 us
  blocking collectives  118 us (43%)
  Pallas kernels  75.7 us (27%)
  starting transfers between devices  48.8 us (18%)
  waiting for transfers between devices  30.8 us (11%)
    all_to_all x10, blocking collectives, swap(): return lax.all_to_all(values, axes, split_axis=0, concat_axis=0, tiled=True)  118 us
    pallas_call x15, Pallas kernels, call(): pl.pallas_call(kernel, out_shape=outs, in_specs=[smem if a.dtype == jnp.i...  75.7 us
    ppermute x20, starting transfers between devices, exchange(): lax.ppermute(values, 'trial', [(i, i ^ k) for i in range(slots)])  30.7 us
    ppermute x20, waiting for transfers between devices, exchange(): lax.ppermute(values, 'trial', [(i, i ^ k) for i in range(slots)])  20.4 us
    all_to_all x3, starting transfers between devices, swap(): return lax.all_to_all(values, axes, split_axis=0, concat_axis=0, tiled=True)  14.2 us
    all_to_all x3, waiting for transfers between devices, swap(): return lax.all_to_all(values, axes, split_axis=0, concat_axis=0, tiled=True)  10.4 us
  transfers between devices with their start and end apart: 25, of which 7 were waited for; matrix products, arithmetic and copies ran while one was open for 0% of the time, Pallas kernels for 8%

commit v1 on v0

--- a/solution.py
+++ b/solution.py
@@ -241,6 +241,7 @@
                 dot3(
                     (high[:, o : o + block], low[:, o : o + block]), (high[:, o:], low[:, o:]), TN
                 )
+                + dot(low[:, o : o + block], low[:, o:], TN)
                 for o in group
             ],
             1,
@@ -502,6 +503,7 @@
     presyn_mine[5] = lax.ppermute(presyn_mine[5], "trial", over)
     ranks = swap(mine, "neuron")
     ranks = ranks.reshape(2, rows, rank_width)
+    rank_g = ranks[0]
     pair = struct((stored, rank_width), bf16)
     blocks = struct((rank_width // 4, 2, rank_width + block), f32)
     weight = learn_rate * norm_rank
@@ -523,11 +525,10 @@
         far=tuple(range(1, 1 + far)),
         far_outs=(0, 1),
     )
-    gram_part, rank_g = lax.optimization_barrier((gram_part, ranks[0]))
+    gram_one = swap(again(swap(gram_part, everyone), neuron_shards * slots), everyone)
+    gram_one, signal_all, rank_g = lax.optimization_barrier((gram_one, signal_all, rank_g))
+    signal_mine = swap(signal_all, "trial")
     rank_g = everywhere(rank_g)
-    gram_one = swap(again(swap(gram_part, everyone), neuron_shards * slots), everyone)
-    gram_one, signal_all = lax.optimization_barrier((gram_one, signal_all))
-    signal_mine = swap(signal_all, "trial")
     square = struct((rank_width, rank_width), bf16)
     upper_hi, upper_lo, right_new = call(
         lambda *r: finish_kernel(math.sqrt(neuron_count), *r),

time: 277 us -> 277 us (level)
  blocking collectives: 118 us -> 138 us
  waiting for transfers between devices: 30.8 us -> 19.5 us
  starting transfers between devices: 48.8 us -> 41.9 us
    all_to_all x10 -> x11, blocking collectives: 118 us -> 138 us  [swap(): return lax.all_to_all(values, axes, split_axis=0, concat_axis=0, tiled=True)]
    ppermute x20, waiting for transfers between devices: 20.4 us -> 10.5 us  [exchange(): lax.ppermute(values, 'trial', [(i, i ^ k) for i in range(slots)])]
    all_to_all x3 -> x2, starting transfers between devices: 14.2 us -> 7.84 us  [swap(): return lax.all_to_all(values, axes, split_axis=0, concat_axis=0, tiled=True)]
    all_to_all x3 -> x2, waiting for transfers between devices: 10.4 us -> 9.02 us  [swap(): return lax.all_to_all(values, axes, split_axis=0, concat_axis=0, tiled=True)]
  transfers between devices with their start and end apart: 25 -> 24, of which waited for: 7 -> 6; matrix products, arithmetic and copies ran while one was open for 0% -> 0% of each run, Pallas kernels for 8% -> 8%
where the time goes in v1:
time: 277 us
  blocking collectives  138 us (50%)
  Pallas kernels  75.3 us (27%)
  starting transfers between devices  41.9 us (15%)
  waiting for transfers between devices  19.5 us (7%)
    all_to_all x11, blocking collectives, swap(): return lax.all_to_all(values, axes, split_axis=0, concat_axis=0, tiled=True)  138 us
    pallas_call x15, Pallas kernels, call(): pl.pallas_call(kernel, out_shape=outs, in_specs=[smem if a.dtype == jnp.i...  75.3 us
    ppermute x20, starting transfers between devices, exchange(): lax.ppermute(values, 'trial', [(i, i ^ k) for i in range(slots)])  30.1 us
    ppermute x20, waiting for transfers between devices, exchange(): lax.ppermute(values, 'trial', [(i, i ^ k) for i in range(slots)])  10.5 us
    all_to_all x2, waiting for transfers between devices, swap(): return lax.all_to_all(values, axes, split_axis=0, concat_axis=0, tiled=True)  9.02 us
    all_to_all x2, starting transfers between devices, swap(): return lax.all_to_all(values, axes, split_axis=0, concat_axis=0, tiled=True)  7.84 us
  transfers between devices with their start and end apart: 24, of which 6 were waited for; matrix products, arithmetic and copies ran while one was open for 0% of the time, Pallas kernels for 8%

profile of v1, /device:TPU:1, one launch (start us, length us, event | category | flops | bytes accessed | tf_op | source)
XLA Modules:
  0.0 276.5 jit_solution(421434759997683291)
XLA Ops:
  0.7 5.4 %start.1 = (f32[16,8192]{1,0:T(8,128)S(1)}, bf16[16,16,512]{2,1,0:T(8,128)(2,1)S(1)}, bf16[8192,512]{1,0:T(8,128)(2,1)S(1)}, bf16[8,16,8192]{2,1,0:T(8,128)(2,1)S(1)}, bf16[8,16,8192]{2,1,0:T(8,128)(2,1)S(1)}) custom-call(s32[1]{0:T(128)} %bitcast.r_0_, f32[1,8192]{1,0:T(1,128)} %bitcast.7, f32[1,8192]{1,0:T(1,128)} %bitcast.16, f32[16,8192]{1,0:T(8,128)} %r_8_.1, ...), custom_call_target="tpu_custom_call" | custom-call | tf_op jit(solution)/shard_map/start/pallas_call | solution.py:369
  6.1 15.9 %all_to_all.65.r_1_ = bf16[16,16,512]{2,1,0:T(8,128)(2,1)S(1)} all-to-all(bf16[16,16,512]{2,1,0:T(8,128)(2,1)S(1)} %get-tuple-element.84), channel_id=1, replica_groups=mesh['neuron'=16,'trial'=8] {'neuron'}, dimensions={0} | all-to-all | bytes 524288 | tf_op jit(solution)/shard_map/all_to_all | solution.py:31
  22.1 5.1 %step.8 = (bf16[8,128,1024]{2,1,0:T(8,128)(2,1)S(1)}, bf16[8,128,1024]{2,1,0:T(8,128)(2,1)S(1)}, f32[16,8192]{1,0:T(8,128)S(1)}, f32[16,8192]{1,0:T(8,128)S(1)},...) custom-call(s32[1]{0:T(128)} %bitcast.r_0_, ...), custom_call_target="tpu_custom_call" | custom-call | tf_op jit(solution)/shard_map/step/pallas_call | solution.py:369
  27.2 10.5 %all_to_all.66.r_1_ = bf16[16,16,512]{2,1,0:T(8,128)(2,1)S(1)} all-to-all(bf16[16,16,512]{2,1,0:T(8,128)(2,1)S(1)} %get-tuple-element.90), channel_id=1, replica_groups=mesh['neuron'=16,'trial'=8] {'neuron'}, dimensions={0} | all-to-all | bytes 524288 | tf_op jit(solution)/shard_map/all_to_all | solution.py:31
  37.7 3.9 %step.9 = (bf16[8,128,1024]{2,1,0:T(8,128)(2,1)S(1)}, bf16[8,128,1024]{2,1,0:T(8,128)(2,1)S(1)}, f32[16,8192]{1,0:T(8,128)S(1)}, f32[16,8192]{1,0:T(8,128)S(1)},...) custom-call(s32[1]{0:T(128)} %bitcast.r_0_, ...), custom_call_target="tpu_custom_call", output_to_operand_aliasing={{0}: (14, {}), {1}: (15, {}), {2}: (8, {}), {3}: (9, {}), {... | custom-call | tf_op jit(solution)/shard_map/step/pallas_call | solution.py:369
  41.6 10.5 %all_to_all.67.r_1_ = bf16[16,16,512]{2,1,0:T(8,128)(2,1)S(1)} all-to-all(bf16[16,16,512]{2,1,0:T(8,128)(2,1)S(1)} %get-tuple-element.97), channel_id=1, replica_groups=mesh['neuron'=16,'trial'=8] {'neuron'}, dimensions={0} | all-to-all | bytes 524288 | tf_op jit(solution)/shard_map/all_to_all | solution.py:31
  52.0 3.9 %step.10 = (bf16[8,128,1024]{2,1,0:T(8,128)(2,1)S(1)}, bf16[8,128,1024]{2,1,0:T(8,128)(2,1)S(1)}, f32[16,8192]{1,0:T(8,128)S(1)}, f32[16,8192]{1,0:T(8,128)S(1)}...) custom-call(s32[1]{0:T(128)} %bitcast.r_0_, ...), custom_call_target="tpu_custom_call", output_to_operand_aliasing={{0}: (14, {}), {1}: (15, {}), {2}: (8, {}), {3}: (9, {}), {... | custom-call | tf_op jit(solution)/shard_map/step/pallas_call | solution.py:369
  55.9 10.2 %all_to_all.68.r_1_ = bf16[16,16,512]{2,1,0:T(8,128)(2,1)S(1)} all-to-all(bf16[16,16,512]{2,1,0:T(8,128)(2,1)S(1)} %get-tuple-element.104), channel_id=1, replica_groups=mesh['neuron'=16,'trial'=8] {'neuron'}, dimensions={0} | all-to-all | bytes 524288 | tf_op jit(solution)/shard_map/all_to_all | solution.py:31
  66.1 3.9 %step.11 = (bf16[8,128,1024]{2,1,0:T(8,128)(2,1)S(1)}, bf16[8,128,1024]{2,1,0:T(8,128)(2,1)S(1)}, f32[16,8192]{1,0:T(8,128)S(1)}, f32[16,8192]{1,0:T(8,128)S(1)}...) custom-call(s32[1]{0:T(128)} %bitcast.r_0_, ...), custom_call_target="tpu_custom_call", output_to_operand_aliasing={{0}: (14, {}), {1}: (15, {}), {2}: (8, {}), {3}: (9, {}), {... | custom-call | tf_op jit(solution)/shard_map/step/pallas_call | solution.py:369
  69.9 10.2 %all_to_all.69.r_1_ = bf16[16,16,512]{2,1,0:T(8,128)(2,1)S(1)} all-to-all(bf16[16,16,512]{2,1,0:T(8,128)(2,1)S(1)} %get-tuple-element.111), channel_id=1, replica_groups=mesh['neuron'=16,'trial'=8] {'neuron'}, dimensions={0} | all-to-all | bytes 524288 | tf_op jit(solution)/shard_map/all_to_all | solution.py:31
  84.0 10.2 %all_to_all.70.r_1_ = bf16[16,16,512]{2,1,0:T(8,128)(2,1)S(1)} all-to-all(bf16[16,16,512]{2,1,0:T(8,128)(2,1)S(1)} %get-tuple-element.118), channel_id=1, replica_groups=mesh['neuron'=16,'trial'=8] {'neuron'}, dimensions={0} | all-to-all | bytes 524288 | tf_op jit(solution)/shard_map/all_to_all | solution.py:31
  98.0 10.2 %all_to_all.71.r_1_ = bf16[16,16,512]{2,1,0:T(8,128)(2,1)S(1)} all-to-all(bf16[16,16,512]{2,1,0:T(8,128)(2,1)S(1)} %get-tuple-element.125), channel_id=1, replica_groups=mesh['neuron'=16,'trial'=8] {'neuron'}, dimensions={0} | all-to-all | bytes 524288 | tf_op jit(solution)/shard_map/all_to_all | solution.py:31
  112.0 10.2 %all_to_all.72.r_1_ = bf16[16,16,512]{2,1,0:T(8,128)(2,1)S(1)} all-to-all(bf16[16,16,512]{2,1,0:T(8,128)(2,1)S(1)} %get-tuple-element.132), channel_id=1, replica_groups=mesh['neuron'=16,'trial'=8] {'neuron'}, dimensions={0} | all-to-all | bytes 524288 | tf_op jit(solution)/shard_map/all_to_all | solution.py:31
  124.7 3.9 %ranks.1 = (bf16[16,16,512]{2,1,0:T(8,128)(2,1)S(1)}, bf16[8,128,1024]{2,1,0:T(8,128)(2,1)}, bf16[128,1024]{1,0:T(8,128)(2,1)}, bf16[128,1024]{1,0:T(8,128)(2,1)...) custom-call(s32[1]{0:T(128)} %bitcast.r_0_, ...), custom_call_target="tpu_custom_call" | custom-call | tf_op jit(solution)/shard_map/ranks/pallas_call | solution.py:369
  132.9 13.1 %collective-permute-start.3 = (bf16[128,1024]{1,0:T(8,128)(2,1)}, bf16[128,1024]{1,0:T(8,128)(2,1)S(1)}, u32[]{:S(2)}, u32[]{:S(2)}) collective-permute-start(bf16[128,1024]{1,0:T(8,128)(2,1)} %get-tuple-element.145), channel_id=1, source_target_pairs={{0,3},{1,2},{2,1},{3,0},{4,7},{5,6},{6,5},{7,4},{8,11},{9,10},{10,... | collective-permute-start | bytes 786440 | tf_op jit(solution)/shard_map/ppermute | solution.py:445
  146.0 10.6 %all_to_all.73.in_ref = bf16[16,16,512]{2,1,0:T(8,128)(2,1)S(1)} all-to-all(bf16[16,16,512]{2,1,0:T(8,128)(2,1)S(1)} %get-tuple-element.141), channel_id=1, replica_groups=mesh['neuron'=16,'trial'=8] {'neuron'}, dimensions={0} | all-to-all | bytes 524288 | tf_op jit(solution)/shard_map/all_to_all | solution.py:31
  165.3 5.6 %all-to-all-done.9 = bf16[16,16,512]{2,1,0:T(8,128)(2,1)S(1)} async-done(((bf16[16,16,512]{2,1,0:T(8,128)(2,1)}), bf16[16,16,512]{2,1,0:T(8,128)(2,1)S(1)}, u32[]{:S(2)}, u32[]{:S(2)}) %all-to-all-start.9) | async-done | bytes 262176 | tf_op jit(solution)/shard_map/all_to_all | solution.py:31
  182.0 4.3 %collective-permute-done.6.r_4_ = bf16[128,512]{1,0:T(8,128)(2,1)S(1)} collective-permute-done((bf16[128,512]{1,0:T(8,128)(2,1)S(1)}, bf16[128,512]{1,0:T(8,128)(2,1)S(1)}, u32[]{:S(2)}, u32[]{:S(2)}) %collective-permute-start.6) | collective-permute-done | bytes 131104 | tf_op jit(solution)/shard_map/ppermute | solution.py:445
  188.3 5.9 %right.1 = (bf16[1024,512]{1,0:T(8,128)(2,1)}, bf16[1024,512]{1,0:T(8,128)(2,1)}, f32[128,2,640]{2,1,0:T(2,128)S(1)}) custom-call(s32[1]{0:T(128)} %bitcast.r_0_, bf16[8192,512]{1,0:T(8,128)(2,1)} %r_1_.1, bf16[128,512]{1,0:T(8,128)(2,1)} %bitcast.50, bf16[128,512]{1,0:T(8,128)(2,1)} %copy-done.23, bf16[128,512]{1,0:T(8,128)(2,1)} %copy-done.20, ...), custom_call_target="tpu_custom_call" | custom-call | tf_op jit(solution)/shard_map/right/pallas_call | solution.py:369
  194.2 20.1 %all_to_all.74.in_ref = f32[128,2,640]{2,1,0:T(2,128)S(1)} all-to-all(f32[128,2,640]{2,1,0:T(2,128)S(1)} %get-tuple-element.156), channel_id=1, replica_groups=mesh['neuron'=16,'trial'=8] {'neuron','trial'}, dimensions={0} | all-to-all | bytes 1310720 | tf_op jit(solution)/shard_map/all_to_all | solution.py:31
  214.7 19.4 %all_to_all.75.r_0_ = f32[128,2,640]{2,1,0:T(2,128)S(1)} all-to-all(f32[128,2,640]{2,1,0:T(2,128)S(1)} %again.3), channel_id=1, replica_groups=mesh['neuron'=16,'trial'=8] {'neuron','trial'}, dimensions={0} | all-to-all | bytes 1310720 | tf_op jit(solution)/shard_map/all_to_all | solution.py:31
  239.0 4.3 %all-to-all-start.12 = ((bf16[8,128,1024]{2,1,0:T(8,128)(2,1)}), bf16[8,128,1024]{2,1,0:T(8,128)(2,1)}, u32[]{:S(2)}, u32[]{:S(2)}) async-start(bf16[8,128,1024]{2,1,0:T(8,128)(2,1)} %get-tuple-element.164), calls=%async_computation.12 | async-start | bytes 4194304 | tf_op jit(solution)/shard_map/all_to_all | solution.py:31
  244.6 21.6 %finish.1 = (bf16[512,512]{1,0:T(8,128)(2,1)S(1)}, bf16[512,512]{1,0:T(8,128)(2,1)S(1)}, bf16[1024,512]{1,0:T(8,128)(2,1)}) custom-call(f32[128,2,640]{2,1,0:T(2,128)S(1)} %all_to_all.75.r_0_, bf16[1024,512]{1,0:T(8,128)(2,1)} %get-tuple-element.159.r_1_, bf16[1024,512]{1,0:T(8,128)(2,1)} %get-tuple-element.160.r_2_), custom_call_target="tpu_custom_call" | custom-call | flops 20000000000 | tf_op jit(solution)/shard_map/finish/pallas_call | solution.py:369
  269.8 6.6 %left.1 = bf16[1024,512]{1,0:T(8,128)(2,1)} custom-call(s32[1]{0:T(128)} %bitcast.r_0_, bf16[512,512]{1,0:T(8,128)(2,1)S(1)} %get-tuple-element.161.r_1_, bf16[512,512]{1,0:T(8,128)(2,1)S(1)} %get-tuple-element.162.r_2_, bf16[8192,512]{1,0:T(8,128)(2,1)} %r_3_.3, bf16[128,512]{1,0:T(8,128)(2,1)} %bitcast.45, bf16[128,512]{1,0:T(8,128)(2,1)} %copy-done.22, ...), custom_call_target="tpu_custom_call" | custom-call | tf_op jit(solution)/shard_map/left/pallas_call | solution.py:369
  (111 shorter events, 50.0 us)
Async XLA Ops:
  128.6 28.8 %collective-permute-start = (bf16[128,1024]{1,0:T(8,128)(2,1)}, bf16[128,1024]{1,0:T(8,128)(2,1)S(1)}, u32[]{:S(2)}, u32[]{:S(2)}) collective-permute-start(bf16[128,1024]{1,0:T(8,128)(2,1)} %get-tuple-element.142), channel_id=1, source_target_pairs={{0,4},{1,5},{2,6},{3,7},{4,0},{5,1},{6,2},{7,3},{8,12},{9,13},{10,... | collective-permute-start | bytes 786440 | tf_op jit(solution)/shard_map/ppermute | solution.py:445
  131.4 26.0 %collective-permute-start.1 = (bf16[128,1024]{1,0:T(8,128)(2,1)}, bf16[128,1024]{1,0:T(8,128)(2,1)S(1)}, u32[]{:S(2)}, u32[]{:S(2)}) collective-permute-start(bf16[128,1024]{1,0:T(8,128)(2,1)} %get-tuple-element.143), channel_id=1, source_target_pairs={{0,6},{1,7},{2,0},{3,1},{4,2},{5,3},{6,4},{7,5},{8,14},{9,15},{10,... | collective-permute-start | bytes 786440 | tf_op jit(solution)/shard_map/ppermute | solution.py:482
  132.3 25.1 %collective-permute-start.2 = (bf16[128,1024]{1,0:T(8,128)(2,1)}, bf16[128,1024]{1,0:T(8,128)(2,1)S(1)}, u32[]{:S(2)}, u32[]{:S(2)}) collective-permute-start(bf16[128,1024]{1,0:T(8,128)(2,1)} %get-tuple-element.144), channel_id=1, source_target_pairs={{0,2},{1,3},{2,0},{3,1},{4,6},{5,7},{6,4},{7,5},{8,10},{9,11},{10,... | collective-permute-start | bytes 786440 | tf_op jit(solution)/shard_map/ppermute | solution.py:445
  132.9 26.0 %collective-permute-start.3 = (bf16[128,1024]{1,0:T(8,128)(2,1)}, bf16[128,1024]{1,0:T(8,128)(2,1)S(1)}, u32[]{:S(2)}, u32[]{:S(2)}) collective-permute-start(bf16[128,1024]{1,0:T(8,128)(2,1)} %get-tuple-element.145), channel_id=1, source_target_pairs={{0,3},{1,2},{2,1},{3,0},{4,7},{5,6},{6,5},{7,4},{8,11},{9,10},{10,... | collective-permute-start | bytes 786440 | tf_op jit(solution)/shard_map/ppermute | solution.py:445
  146.0 12.9 %collective-permute-start.4 = (bf16[128,1024]{1,0:T(8,128)(2,1)}, bf16[128,1024]{1,0:T(8,128)(2,1)S(1)}, u32[]{:S(2)}, u32[]{:S(2)}) collective-permute-start(bf16[128,1024]{1,0:T(8,128)(2,1)} %get-tuple-element.146), channel_id=1, source_target_pairs={{0,6},{1,7},{2,4},{3,5},{4,2},{5,3},{6,0},{7,1},{8,14},{9,15},{10,... | collective-permute-start | bytes 786440 | tf_op jit(solution)/shard_map/ppermute | solution.py:445
  158.9 12.0 %all-to-all-start.9 = ((bf16[16,16,512]{2,1,0:T(8,128)(2,1)}), bf16[16,16,512]{2,1,0:T(8,128)(2,1)S(1)}, u32[]{:S(2)}, u32[]{:S(2)}) async-start(bf16[16,16,512]{2,1,0:T(8,128)(2,1)} %again.2), calls=%async_computation.9 | async-start | bytes 524288 | tf_op jit(solution)/shard_map/all_to_all | solution.py:31
  162.5 13.1 %collective-permute-start.12 = (bf16[128,1024]{1,0:T(8,128)(2,1)}, bf16[128,1024]{1,0:T(8,128)(2,1)S(1)}, u32[]{:S(2)}, u32[]{:S(2)}) collective-permute-start(bf16[128,1024]{1,0:T(8,128)(2,1)} %get-tuple-element.149), channel_id=1, source_target_pairs={{0,1},{1,0},{2,3},{3,2},{4,5},{5,4},{6,7},{7,6},{8,9},{9,8},{10,11... | collective-permute-start | bytes 786440 | tf_op jit(solution)/shard_map/ppermute | solution.py:445
  162.7 13.1 %collective-permute-start.14 = (bf16[128,1024]{1,0:T(8,128)(2,1)}, bf16[128,1024]{1,0:T(8,128)(2,1)S(1)}, u32[]{:S(2)}, u32[]{:S(2)}) collective-permute-start(bf16[128,1024]{1,0:T(8,128)(2,1)} %get-tuple-element.155), channel_id=1, source_target_pairs={{0,7},{1,6},{2,5},{3,4},{4,3},{5,2},{6,1},{7,0},{8,15},{9,14},{10,... | collective-permute-start | bytes 786440 | tf_op jit(solution)/shard_map/ppermute | solution.py:445
  171.0 5.3 %collective-permute-start.10 = (bf16[128,512]{1,0:T(8,128)(2,1)S(1)}, bf16[128,512]{1,0:T(8,128)(2,1)S(1)}, u32[]{:S(2)}, u32[]{:S(2)}) collective-permute-start(bf16[128,512]{1,0:T(8,128)(2,1)S(1)} %bitcast.46), channel_id=1, source_target_pairs={{0,6},{1,7},{2,4},{3,5},{4,2},{5,3},{6,0},{7,1},{8,14},{9,15},{10,... | collective-permute-start | bytes 393224 | tf_op jit(solution)/shard_map/ppermute | solution.py:445
  171.9 14.3 %collective-permute-start.13 = (bf16[128,1024]{1,0:T(8,128)(2,1)S(1)}, bf16[128,1024]{1,0:T(8,128)(2,1)S(1)}, u32[]{:S(2)}, u32[]{:S(2)}) collective-permute-start(bf16[128,1024]{1,0:T(8,128)(2,1)S(1)} %collective-permute-done.1), channel_id=1, source_target_pairs={{0,7},{1,6},{2,1},{3,0},{4,3},{5,2},{6,5},{7,4},{8,15},{9,14},{10,... | collective-permute-start | bytes 786440 | tf_op jit(solution)/shard_map/ppermute | solution.py:503
  175.1 6.7 %collective-permute-start.8 = (bf16[128,512]{1,0:T(8,128)(2,1)S(1)}, bf16[128,512]{1,0:T(8,128)(2,1)S(1)}, u32[]{:S(2)}, u32[]{:S(2)}) collective-permute-start(bf16[128,512]{1,0:T(8,128)(2,1)S(1)} %bitcast.47), channel_id=1, source_target_pairs={{0,4},{1,5},{2,6},{3,7},{4,0},{5,1},{6,2},{7,3},{8,12},{9,13},{10,... | collective-permute-start | bytes 393224 | tf_op jit(solution)/shard_map/ppermute | solution.py:445
  175.6 10.7 %collective-permute-start.6 = (bf16[128,512]{1,0:T(8,128)(2,1)S(1)}, bf16[128,512]{1,0:T(8,128)(2,1)S(1)}, u32[]{:S(2)}, u32[]{:S(2)}) collective-permute-start(bf16[128,512]{1,0:T(8,128)(2,1)S(1)} %bitcast.48), channel_id=1, source_target_pairs={{0,2},{1,3},{2,0},{3,1},{4,6},{5,7},{6,4},{7,5},{8,10},{9,11},{10,... | collective-permute-start | bytes 393224 | tf_op jit(solution)/shard_map/ppermute | solution.py:445
  175.8 10.5 %collective-permute-start.5 = (bf16[128,512]{1,0:T(8,128)(2,1)S(1)}, bf16[128,512]{1,0:T(8,128)(2,1)S(1)}, u32[]{:S(2)}, u32[]{:S(2)}) collective-permute-start(bf16[128,512]{1,0:T(8,128)(2,1)S(1)} %bitcast.49), channel_id=1, source_target_pairs={{0,1},{1,0},{2,3},{3,2},{4,5},{5,4},{6,7},{7,6},{8,9},{9,8},{10,11... | collective-permute-start | bytes 393224 | tf_op jit(solution)/shard_map/ppermute | solution.py:445
  176.3 10.0 %collective-permute-start.11 = (bf16[128,512]{1,0:T(8,128)(2,1)S(1)}, bf16[128,512]{1,0:T(8,128)(2,1)S(1)}, u32[]{:S(2)}, u32[]{:S(2)}) collective-permute-start(bf16[128,512]{1,0:T(8,128)(2,1)S(1)} %collective-permute-done.10.r_8_), channel_id=1, source_target_pairs={{0,1},{1,0},{2,3},{3,2},{4,5},{5,4},{6,7},{7,6},{8,9},{9,8},{10,11... | collective-permute-start | bytes 393224 | tf_op jit(solution)/shard_map/ppermute | solution.py:445
  181.8 4.5 %collective-permute-start.9 = (bf16[128,512]{1,0:T(8,128)(2,1)S(1)}, bf16[128,512]{1,0:T(8,128)(2,1)S(1)}, u32[]{:S(2)}, u32[]{:S(2)}) collective-permute-start(bf16[128,512]{1,0:T(8,128)(2,1)S(1)} %collective-permute-done.8.r_6_), channel_id=1, source_target_pairs={{0,1},{1,0},{2,3},{3,2},{4,5},{5,4},{6,7},{7,6},{8,9},{9,8},{10,11... | collective-permute-start | bytes 393224 | tf_op jit(solution)/shard_map/ppermute | solution.py:445
  186.3 1.3 collective-permute-start.7
  234.1 9.3 %collective-permute-start.20 = (bf16[128,512]{1,0:T(8,128)(2,1)S(1)}, bf16[128,512]{1,0:T(8,128)(2,1)S(1)}, u32[]{:S(2)}, u32[]{:S(2)}) collective-permute-start(bf16[128,512]{1,0:T(8,128)(2,1)S(1)} %bitcast.41), channel_id=1, source_target_pairs={{0,6},{1,7},{2,4},{3,5},{4,2},{5,3},{6,0},{7,1},{8,14},{9,15},{10,... | collective-permute-start | bytes 393224 | tf_op jit(solution)/shard_map/ppermute | solution.py:445
  234.9 9.1 %collective-permute-start.18 = (bf16[128,512]{1,0:T(8,128)(2,1)S(1)}, bf16[128,512]{1,0:T(8,128)(2,1)S(1)}, u32[]{:S(2)}, u32[]{:S(2)}) collective-permute-start(bf16[128,512]{1,0:T(8,128)(2,1)S(1)} %bitcast.42), channel_id=1, source_target_pairs={{0,4},{1,5},{2,6},{3,7},{4,0},{5,1},{6,2},{7,3},{8,12},{9,13},{10,... | collective-permute-start | bytes 393224 | tf_op jit(solution)/shard_map/ppermute | solution.py:445
  235.9 8.2 %collective-permute-start.16 = (bf16[128,512]{1,0:T(8,128)(2,1)S(1)}, bf16[128,512]{1,0:T(8,128)(2,1)S(1)}, u32[]{:S(2)}, u32[]{:S(2)}) collective-permute-start(bf16[128,512]{1,0:T(8,128)(2,1)S(1)} %bitcast.43), channel_id=1, source_target_pairs={{0,2},{1,3},{2,0},{3,1},{4,6},{5,7},{6,4},{7,5},{8,10},{9,11},{10,... | collective-permute-start | bytes 393224 | tf_op jit(solution)/shard_map/ppermute | solution.py:445
  237.3 28.9 %collective-permute-start.15 = (bf16[128,512]{1,0:T(8,128)(2,1)S(1)}, bf16[128,512]{1,0:T(8,128)(2,1)S(1)}, u32[]{:S(2)}, u32[]{:S(2)}) collective-permute-start(bf16[128,512]{1,0:T(8,128)(2,1)S(1)} %bitcast.44), channel_id=1, source_target_pairs={{0,1},{1,0},{2,3},{3,2},{4,5},{5,4},{6,7},{7,6},{8,9},{9,8},{10,11... | collective-permute-start | bytes 393224 | tf_op jit(solution)/shard_map/ppermute | solution.py:445
  239.0 30.7 %all-to-all-start.12 = ((bf16[8,128,1024]{2,1,0:T(8,128)(2,1)}), bf16[8,128,1024]{2,1,0:T(8,128)(2,1)}, u32[]{:S(2)}, u32[]{:S(2)}) async-start(bf16[8,128,1024]{2,1,0:T(8,128)(2,1)} %get-tuple-element.164), calls=%async_computation.12 | async-start | bytes 4194304 | tf_op jit(solution)/shard_map/all_to_all | solution.py:31
  243.4 22.9 %collective-permute-start.21 = (bf16[128,512]{1,0:T(8,128)(2,1)S(1)}, bf16[128,512]{1,0:T(8,128)(2,1)S(1)}, u32[]{:S(2)}, u32[]{:S(2)}) collective-permute-start(bf16[128,512]{1,0:T(8,128)(2,1)S(1)} %collective-permute-done.20.r_10_), channel_id=1, source_target_pairs={{0,1},{1,0},{2,3},{3,2},{4,5},{5,4},{6,7},{7,6},{8,9},{9,8},{10,11... | collective-permute-start | bytes 393224 | tf_op jit(solution)/shard_map/ppermute | solution.py:445
  244.0 22.3 %collective-permute-start.19 = (bf16[128,512]{1,0:T(8,128)(2,1)S(1)}, bf16[128,512]{1,0:T(8,128)(2,1)S(1)}, u32[]{:S(2)}, u32[]{:S(2)}) collective-permute-start(bf16[128,512]{1,0:T(8,128)(2,1)S(1)} %collective-permute-done.18.r_8_), channel_id=1, source_target_pairs={{0,1},{1,0},{2,3},{3,2},{4,5},{5,4},{6,7},{7,6},{8,9},{9,8},{10,11... | collective-permute-start | bytes 393224 | tf_op jit(solution)/shard_map/ppermute | solution.py:445
  244.1 22.2 %collective-permute-start.17 = (bf16[128,512]{1,0:T(8,128)(2,1)S(1)}, bf16[128,512]{1,0:T(8,128)(2,1)S(1)}, u32[]{:S(2)}, u32[]{:S(2)}) collective-permute-start(bf16[128,512]{1,0:T(8,128)(2,1)S(1)} %collective-permute-done.16.r_6_), channel_id=1, source_target_pairs={{0,1},{1,0},{2,3},{3,2},{4,5},{5,4},{6,7},{7,6},{8,9},{9,8},{10,11... | collective-permute-start | bytes 393224 | tf_op jit(solution)/shard_map/ppermute | solution.py:445
  (30 other events, 480.4 us)
